TPU v7x, 512 devices: a whole 4x4x16 slice. The times are simulated.
512 devices in a mesh: feat: 64 (over x, z), dom: 8 (over y, core).
Axes of the slice: x: 4, y: 4, z: 16, core: 2. Of those that a mesh axis runs over, the one named last changes fastest.
Arguments:
- features: bfloat16 [65536, 1024], P('dom', 'feat'), may hold values from -6 to 6
- self_weight: bfloat16 [1024, 512], P('feat'), may hold values from -0.1875 to 0.1875
- neighbour_weight: bfloat16 [1024, 512], P('feat'), may hold values from -1.5 to 1.5
- cotangent: bfloat16 [65536, 512], P(('dom', 'feat')), may hold values from -0.09375 to 0.09375
- send_rows: int32 [8, 8, 256], replicated, may hold values from 0 to 8191
- send_count: int32 [8, 8], replicated, may hold values from 32 to 256, as said below
- tile_source: int32 [8, 64, 8], P('dom'), may hold values from 0 to 79
- tile_kind: int32 [8, 64, 8], P('dom'), may hold values from 0 to 63
- tile_patterns: bfloat16 [64, 128, 128], replicated, may hold values from 0.0099487305 to 1
Outputs:
- hidden: bfloat16 [65536, 512], P(('dom', 'feat'))
- grad_self: float32 [1024, 512], P('feat')
- grad_neighbour: float32 [1024, 512], P('feat')
Inputs may be any that keep to these rules, and one draw needn't show every extreme that they name: `send_count`: one destination has 256 live slots from every owner.
All inputs are finite; a program needn't handle non-finite values.
Results may differ from a plain program's by a relative error of at most 0.005.
Values may be sent and summed in bfloat16 or wider, within the bound.
A program may use at most 128 MiB of HBM per device.

v0:
```python
import jax
import jax.numpy as jnp
from jax import lax
from jax.sharding import PartitionSpec as P

inv_root_two = 0.7071067811865476
inv_root_two_pi = 0.3989422804014327


def gelu_pair(linear):
    normal_cdf = 0.5 * (1.0 + jax.scipy.special.erf(linear * inv_root_two))
    density = jnp.exp(-0.5 * linear * linear) * inv_root_two_pi
    return (linear * normal_cdf, normal_cdf + linear * density)


def on_device(
    features,
    self_weight,
    neighbour_weight,
    cotangent,
    send_rows,
    send_count,
    tile_source,
    tile_kind,
    tile_patterns,
):
    my_part = lax.axis_index("dom")
    part_count = lax.axis_size("dom")
    row_count = features.shape[0]
    col_count = features.shape[1]
    slot_count = send_rows.shape[2]
    tile_rows = tile_patterns.shape[1]
    slot_ids = jnp.arange(slot_count, dtype=jnp.int32)
    everything = lax.all_gather(features, "dom", axis=0, tiled=True)
    wanted = lax.dynamic_index_in_dim(send_rows, my_part, 1, keepdims=False)
    counts = lax.dynamic_index_in_dim(send_count, my_part, 1, keepdims=False)
    flat_ids = jnp.arange(part_count, dtype=jnp.int32)[:, None] * row_count + wanted
    remote = everything[flat_ids.reshape(-1)].reshape(part_count, slot_count, col_count)
    live_mask = slot_ids[None, :] < counts[:, None]
    remote = jnp.where(live_mask[:, :, None], remote, jnp.zeros((), jnp.bfloat16))
    extended = jnp.concatenate([features, remote.reshape(-1, col_count)], 0).reshape(
        -1, tile_rows, col_count
    )
    kinds = tile_kind[0]
    tile_mats = tile_patterns[kinds]
    sources = extended[tile_source[0]]
    summed = jnp.einsum("tkab,tkbf->taf", tile_mats, sources, preferred_element_type=jnp.float32)
    pattern_sums = jnp.sum(tile_patterns, axis=2, dtype=jnp.float32)
    degree = jnp.sum(pattern_sums[kinds], axis=1)
    neighbour_mean = (
        (summed / degree[:, :, None]).reshape(row_count, col_count).astype(jnp.bfloat16)
    )
    own_features, own_mean = (
        lax.all_to_all(features, "feat", split_axis=0, concat_axis=1, tiled=True),
        lax.all_to_all(neighbour_mean, "feat", split_axis=0, concat_axis=1, tiled=True),
    )
    linear = jnp.dot(
        own_features,
        lax.all_gather(self_weight, "feat", axis=0, tiled=True),
        preferred_element_type=jnp.float32,
    ) + jnp.dot(
        own_mean,
        lax.all_gather(neighbour_weight, "feat", axis=0, tiled=True),
        preferred_element_type=jnp.float32,
    )
    gelu_value, gelu_slope = gelu_pair(linear)
    hidden = gelu_value.astype(jnp.bfloat16)
    grad_linear = (cotangent.astype(jnp.float32) * gelu_slope).astype(jnp.bfloat16)
    shard_rows = lax.all_gather(grad_linear, "feat", axis=0, tiled=True)
    self_part = jnp.einsum("rc,rh->ch", features, shard_rows, preferred_element_type=jnp.float32)
    neigh_part = jnp.einsum(
        "rc,rh->ch", neighbour_mean, shard_rows, preferred_element_type=jnp.float32
    )
    self_local, neigh_local = (self_part, neigh_part)
    grad_self, grad_neighbour = lax.psum((self_local, neigh_local), "dom")
    return (hidden, grad_self, grad_neighbour)


def solution(mesh):
    placed = (
        P("dom", "feat"),
        P("feat", None),
        P("feat", None),
        P(("dom", "feat"), None),
        P(),
        P(),
        P("dom", None, None),
        P("dom", None, None),
        P(),
    )
    return jax.shard_map(
        on_device,
        mesh=mesh,
        in_specs=placed,
        out_specs=(P(("dom", "feat"), None), P("feat", None), P("feat", None)),
        check_vma=False,
    )
```

profile of v0, /device:TPU:2, one launch (start us, length us, event | category | flops | bytes accessed | tf_op | source)
XLA Modules:
  0.0 632.6 jit_solution(4560406625717011600)
XLA Ops:
  7.2 0.0 copy-start
  7.2 0.0 copy-start.1
  7.2 0.0 all-gather.7.cloned.1.call-start
  7.2 2.7 copy.29
  10.0 0.0 all-gather.7.cloned.1.call-update
  10.0 0.0 all-gather.5.cloned.1.call-start
  10.1 0.7 all-gather.5.cloned.1.call-update
  10.8 1.7 copy_bitcast_fusion.1
  12.5 18.6 %all-to-all-start = ((bf16[64,128,16]{1,2,0:T(8,128)(2,1)}), bf16[64,128,16]{1,2,0:T(8,128)(2,1)S(1)}, u32[]{:S(2)}, u32[]{:S(2)}) async-start(bf16[64,128,16]{1,2,0:T(8,128)(2,1)} %copy_bitcast_fusion.1), calls=%async_computation | async-start | bytes 524288 | tf_op jit(solution)/shard_map/all_to_all | solution.py:54
  31.1 0.0 all-gather.9.cloned.1.call-start
  31.2 0.7 all-gather.9.cloned.1.call-update
  31.9 0.1 broadcast_bitcast_fusion
  32.0 0.9 dynamic-slice_reduce_fusion
  32.9 0.1 iota_compare_fusion
  33.0 0.7 compare_select_fusion.1
  33.7 0.1 copy.31
  33.8 0.1 reshape.150
  33.9 0.7 compare_select_fusion.2
  34.6 0.1 copy.28
  34.7 0.1 reshape.134
  34.8 2.5 convert_reduce_fusion
  37.3 14.0 %gather_fusion = bf16[512,128,128]{2,1,0:T(8,128)(2,1)} fusion(bf16[64,128,128]{2,1,0:T(8,128)(2,1)S(1)} %copy-done.1, s32[1024]{0:T(1024)S(1)} %pad_clamp_fusion.1), kind=kCustom, calls=%fused_computation | custom fusion | bytes 33556480 | tf_op jit(solution)/shard_map/gather | solution.py:45
  51.3 1.0 gather_fusion.3
  52.3 0.1 bitcast_reduce_fusion
  52.4 54.8 %all-gather.7.cloned.1.call-done = bf16[65536,16]{1,0:T(8,128)(2,1)} async-done(((bf16[8192,16]{1,0:T(8,128)(2,1)}), bf16[65536,16]{1,0:T(8,128)(2,1)}) %all-gather.7.cloned.1.call-update) | async-done | bytes 2097168 | tf_op jit(solution)/shard_map/all_gather | solution.py:34
  107.2 13.5 %gather_fusion.1 = bf16[2048,16]{1,0:T(8,128)(2,1)S(1)} fusion(bf16[65536,16]{1,0:T(8,128)(2,1)} %all-gather.7.cloned.1.call-done, s32[2048]{0:T(1024)S(1)} %broadcast_clamp_fusion), kind=kCustom, calls=%fused_computation.1 | custom fusion | bytes 139264 | tf_op jit(solution)/shard_map/gather | solution.py:38
  120.8 0.3 broadcast_select_fusion
  121.1 0.2 copy.30
  121.3 0.1 copy_bitcast_fusion
  121.4 2.0 gather_fusion.2
  123.4 0.0 copy-start.4
  123.4 8.9 %fusion.1 = bf16[64,128,16]{1,2,0:T(8,128)(2,1)} fusion(bf16[64,8,128,128]{3,2,1,0:T(8,128)(2,1)} %bitcast.61, bf16[64,8,128,16]{2,3,1,0:T(8,128)(2,1)S(1)} %bitcast.60, f32[64,128]{1,0:T(8,128)S(1)} %bitcast_reduce_fusion), kind=kOutput, calls=%fused_computation.9 | convolution fusion | flops 268697600 | bytes 19169280 | tf_op jit(solution)/shard_map/tkab,tkbf->taf/dot_general | solution.py:47
  132.3 15.7 %all-to-all-start.1 = ((bf16[64,128,16]{1,2,0:T(8,128)(2,1)}), bf16[64,128,16]{1,2,0:T(8,128)(2,1)S(1)}, u32[]{:S(2)}, u32[]{:S(2)}) async-start(bf16[64,128,16]{1,2,0:T(8,128)(2,1)} %fusion.1), calls=%async_computation.1 | async-start | bytes 524288 | tf_op jit(solution)/shard_map/all_to_all | solution.py:55
  148.0 0.0 all-gather.11.cloned.1.call-start
  148.0 102.2 %all-gather.5.cloned.1.call-done = bf16[1024,512]{1,0:T(8,128)(2,1)} async-done(((bf16[16,512]{1,0:T(8,128)(2,1)}), bf16[1024,512]{1,0:T(8,128)(2,1)}) %all-gather.5.cloned.1.call-update) | async-done | bytes 1048592 | tf_op jit(solution)/shard_map/all_gather | solution.py:59
  250.2 1.5 fusion.11
  251.8 137.4 %all-gather.9.cloned.1.call-done = bf16[1024,512]{1,0:T(8,128)(2,1)} async-done(((bf16[16,512]{1,0:T(8,128)(2,1)}), bf16[1024,512]{1,0:T(8,128)(2,1)}) %all-gather.9.cloned.1.call-update) | async-done | bytes 1048592 | tf_op jit(solution)/shard_map/all_gather | solution.py:63
  389.2 2.3 fusion.7
  391.5 0.0 all-gather.11.cloned.1.call-update
  391.5 0.0 all-reduce.3.cloned.1.call-start
  391.6 152.3 %all-gather.11.cloned.1.call-done = bf16[8192,512]{1,0:T(8,128)(2,1)} async-done(((bf16[128,512]{1,0:T(8,128)(2,1)}), bf16[8192,512]{1,0:T(8,128)(2,1)}) %all-gather.11.cloned.1.call-update) | async-done | bytes 8388624 | tf_op jit(solution)/shard_map/all_gather | solution.py:69
  543.9 5.4 fusion.8
  549.3 0.4 copy-done.2
  549.7 1.8 convolution_bitcast_fusion.1
  551.5 0.0 all-reduce.3.cloned.1.call-update
  551.6 71.8 %all-reduce.3.cloned.1.call-done = (f32[16,512]{1,0:T(8,128)}, f32[16,512]{1,0:T(8,128)}) async-done(((f32[16,512]{1,0:T(8,128)}, f32[16,512]{1,0:T(8,128)}), (f32[16,512]{1,0:T(8,128)}, f32[16,512]{1,0:T(8,128)})) %all-reduce.3.cloned.1.call-update) | async-done | bytes 65552 | tf_op jit(solution)/shard_map/psum | solution.py:75
  623.3 1.4 copy.47
  624.7 1.4 copy.48
  (16 shorter events, 0.1 us)
Async XLA Ops:
  7.2 24.8 %copy-start = (s32[8,8,256]{2,1,0:T(8,128)S(1)}, s32[8,8,256]{2,1,0:T(8,128)}, u32[]{:S(2)}) copy-start(s32[8,8,256]{2,1,0:T(8,128)} %param.13) | copy-start | bytes 196612
  7.2 30.1 %copy-start.1 = (bf16[64,128,128]{2,1,0:T(8,128)(2,1)S(1)}, bf16[64,128,128]{2,1,0:T(8,128)(2,1)}, u32[]{:S(2)}) copy-start(bf16[64,128,128]{2,1,0:T(8,128)(2,1)} %param.17) | copy-start | bytes 6291460
  7.2 100.0 %all-gather.7.cloned.1.call-start = ((), (), s32[]{:S(2)}) async-start(), calls=%async_computation.3 | async-start | bytes 18874368 | tf_op jit(solution)/shard_map/all_gather | solution.py:34
  10.0 240.2 %all-gather.5.cloned.1.call-start = ((), (), s32[]{:S(2)}) async-start(), calls=%async_computation.2 | async-start | bytes 1064960 | tf_op jit(solution)/shard_map/all_gather | solution.py:59
  12.5 119.8 %all-to-all-start = ((bf16[64,128,16]{1,2,0:T(8,128)(2,1)}), bf16[64,128,16]{1,2,0:T(8,128)(2,1)S(1)}, u32[]{:S(2)}, u32[]{:S(2)}) async-start(bf16[64,128,16]{1,2,0:T(8,128)(2,1)} %copy_bitcast_fusion.1), calls=%async_computation | async-start | bytes 524288 | tf_op jit(solution)/shard_map/all_to_all | solution.py:54
  31.1 358.1 %all-gather.9.cloned.1.call-start = ((), (), s32[]{:S(2)}) async-start(), calls=%async_computation.4 | async-start | bytes 1064960 | tf_op jit(solution)/shard_map/all_gather | solution.py:63
  51.3 70.0 %copy-start.3 = (bf16[8192,16]{0,1:T(8,128)(2,1)S(1)}, bf16[8192,16]{0,1:T(8,128)(2,1)}, u32[]{:S(2)}) copy-start(bf16[8192,16]{0,1:T(8,128)(2,1)} %param.9) | copy-start | bytes 786436
  123.4 265.8 %copy-start.4 = (bf16[128,512]{1,0:T(8,128)(2,1)S(1)}, bf16[128,512]{1,0:T(8,128)(2,1)}, u32[]{:S(2)}) copy-start(bf16[128,512]{1,0:T(8,128)(2,1)} %param.12) | copy-start | bytes 393220
  132.3 256.9 %all-to-all-start.1 = ((bf16[64,128,16]{1,2,0:T(8,128)(2,1)}), bf16[64,128,16]{1,2,0:T(8,128)(2,1)S(1)}, u32[]{:S(2)}, u32[]{:S(2)}) async-start(bf16[64,128,16]{1,2,0:T(8,128)(2,1)} %fusion.1), calls=%async_computation.1 | async-start | bytes 524288 | tf_op jit(solution)/shard_map/all_to_all | solution.py:55
  148.0 395.9 %all-gather.11.cloned.1.call-start = ((), (), s32[]{:S(2)}) async-start(), calls=%async_computation.5 | async-start | bytes 8519680 | tf_op jit(solution)/shard_map/all_gather | solution.py:69
  391.5 231.8 %all-reduce.3.cloned.1.call-start = ((), (), s32[]{:S(2)}) async-start(), calls=%async_computation.6 | async-start | bytes 131072 | tf_op jit(solution)/shard_map/psum | solution.py:75
  543.9 5.9 copy-start.2
Sparse Core Ops, SparseCore 0:
  10.2 97.0 all-gather.6
  110.2 140.0 all-gather.4
  253.2 135.9 all-gather.8
  392.0 151.8 all-gather.10
  551.7 71.6 all-reduce.2
where the time goes:
time: 633 us
  waiting for transfers between devices  520 us (82%)
  local copies, waits for them, and re-layouts  39.7 us (6%)
  starting transfers between devices  34.6 us (5%)
  matrix products  20 us (3%)
  between operations  13.9 us (2%)
    all_gather x1, waiting for transfers between devices, on_device(): shard_rows = lax.all_gather(grad_linear, 'feat', axis=0, tiled=True)  152 us
    all_gather x1, waiting for transfers between devices, on_device(): lax.all_gather(neighbour_weight, 'feat', axis=0, tiled=True)  137 us
    all_gather x1, waiting for transfers between devices, on_device(): lax.all_gather(self_weight, 'feat', axis=0, tiled=True)  102 us
    psum x1, waiting for transfers between devices, on_device(): grad_self, grad_neighbour = lax.psum((self_local, neigh_local), 'dom')  71.8 us
    all_gather x1, waiting for transfers between devices, on_device(): everything = lax.all_gather(features, 'dom', axis=0, tiled=True)  54.8 us
    all_to_all x1, starting transfers between devices, on_device(): lax.all_to_all(features, 'feat', split_axis=0, concat_axis=1, tiled=True)  18.6 us
    all_to_all x1, starting transfers between devices, on_device(): lax.all_to_all(neighbour_mean, 'feat', split_axis=0, concat_axis=1, tiled...  15.7 us
    gather x1, local copies, waits for them, and re-layouts, on_device(): tile_mats = tile_patterns[kinds]  14 us
  transfers between devices with their start and end apart: 7, of which 5 were waited for; matrix products, arithmetic and copies ran while one was open for 8% of the time, Pallas kernels for 0%

commit v1 on v0

--- a/solution.py
+++ b/solution.py
@@ -5,6 +5,11 @@
 
 inv_root_two = 0.7071067811865476
 inv_root_two_pi = 0.3989422804014327
+
+
+def swapped_in(shard, axis, dim):
+    sent = jnp.stack([shard] * lax.axis_size(axis))
+    return jnp.concatenate(lax.all_to_all(sent, axis, 0, 0), axis=dim)
 
 
 def gelu_pair(linear):
@@ -66,7 +71,7 @@
     gelu_value, gelu_slope = gelu_pair(linear)
     hidden = gelu_value.astype(jnp.bfloat16)
     grad_linear = (cotangent.astype(jnp.float32) * gelu_slope).astype(jnp.bfloat16)
-    shard_rows = lax.all_gather(grad_linear, "feat", axis=0, tiled=True)
+    shard_rows = swapped_in(grad_linear, "feat", 0)
     self_part = jnp.einsum("rc,rh->ch", features, shard_rows, preferred_element_type=jnp.float32)
     neigh_part = jnp.einsum(
         "rc,rh->ch", neighbour_mean, shard_rows, preferred_element_type=jnp.float32

time: 633 us -> 844 us (1.33)
  blocking collectives: 0 us -> 365 us
  waiting for transfers between devices: 520 us -> 367 us
    all_to_all x0 -> x1, blocking collectives: none -> 365 us  [swapped_in(): return jnp.concatenate(lax.all_to_all(sent, axis, 0, 0), axis=dim)]
    all_gather x1 -> x0, waiting for transfers between devices: 152 us -> none  [on_device(): shard_rows = lax.all_gather(grad_linear, 'feat', axis=0, tiled=True)]
  transfers between devices with their start and end apart: 7 -> 6, of which waited for: 5 -> 4; matrix products, arithmetic and copies ran while one was open for 8% -> 6% of each run, Pallas kernels for 0% -> 0%
where the time goes in v1:
time: 844 us; the launch traced here: 843 us
  waiting for transfers between devices  367 us (43%)
  blocking collectives  365 us (43%)
  local copies, waits for them, and re-layouts  40.3 us (5%)
  starting transfers between devices  34.7 us (4%)
  matrix products  17.3 us (2%)
  between operations  13.9 us (2%)
    all_to_all x1, blocking collectives, swapped_in(): return jnp.concatenate(lax.all_to_all(sent, axis, 0, 0), axis=dim)  365 us
    all_gather x1, waiting for transfers between devices, on_device(): lax.all_gather(neighbour_weight, 'feat', axis=0, tiled=True)  137 us
    all_gather x1, waiting for transfers between devices, on_device(): lax.all_gather(self_weight, 'feat', axis=0, tiled=True)  102 us
    psum x1, waiting for transfers between devices, on_device(): grad_self, grad_neighbour = lax.psum((self_local, neigh_local), 'dom')  71.3 us
    all_gather x1, waiting for transfers between devices, on_device(): everything = lax.all_gather(features, 'dom', axis=0, tiled=True)  54.7 us
    all_to_all x1, starting transfers between devices, on_device(): lax.all_to_all(features, 'feat', split_axis=0, concat_axis=1, tiled=True)  18.6 us
  transfers between devices with their start and end apart: 6, of which 4 were waited for; matrix products, arithmetic and copies ran while one was open for 6% of the time, Pallas kernels for 0%

profile of v1, /device:TPU:2, one launch (start us, length us, event | category | flops | bytes accessed | tf_op | source)
XLA Modules:
  0.0 843.1 jit_solution(14438376030110432339)
XLA Ops:
  7.2 0.0 copy-start
  7.2 0.0 copy-start.1
  7.2 0.0 all-gather.6.cloned.1.call-start
  7.2 2.8 copy.27
  10.0 0.0 all-gather.6.cloned.1.call-update
  10.0 0.0 all-gather.4.cloned.1.call-start
  10.1 0.7 all-gather.4.cloned.1.call-update
  10.8 1.7 copy_bitcast_fusion.1
  12.5 18.6 %all-to-all-start = ((bf16[64,128,16]{1,2,0:T(8,128)(2,1)}), bf16[64,128,16]{1,2,0:T(8,128)(2,1)S(1)}, u32[]{:S(2)}, u32[]{:S(2)}) async-start(bf16[64,128,16]{1,2,0:T(8,128)(2,1)} %copy_bitcast_fusion.1), calls=%async_computation | async-start | bytes 524288 | tf_op jit(solution)/shard_map/all_to_all | solution.py:59
  31.1 0.0 all-gather.8.cloned.1.call-start
  31.2 0.7 all-gather.8.cloned.1.call-update
  31.9 0.1 broadcast_bitcast_fusion
  32.0 0.9 dynamic-slice_reduce_fusion
  32.9 0.1 iota_compare_fusion
  33.0 0.7 compare_select_fusion.1
  33.7 0.1 copy.29
  33.8 0.1 reshape.156
  33.9 0.7 compare_select_fusion.2
  34.6 0.1 copy.26
  34.7 0.1 reshape.140
  34.8 2.6 convert_reduce_fusion
  37.4 14.0 %gather_fusion = bf16[512,128,128]{2,1,0:T(8,128)(2,1)} fusion(bf16[64,128,128]{2,1,0:T(8,128)(2,1)S(1)} %copy-done.1, s32[1024]{0:T(1024)S(1)} %pad_clamp_fusion.1), kind=kCustom, calls=%fused_computation | custom fusion | bytes 33556480 | tf_op jit(solution)/shard_map/gather | solution.py:50
  51.4 1.0 gather_fusion.3
  52.4 0.1 bitcast_reduce_fusion
  52.5 54.7 %all-gather.6.cloned.1.call-done = bf16[65536,16]{1,0:T(8,128)(2,1)} async-done(((bf16[8192,16]{1,0:T(8,128)(2,1)}), bf16[65536,16]{1,0:T(8,128)(2,1)}) %all-gather.6.cloned.1.call-update) | async-done | bytes 2097168 | tf_op jit(solution)/shard_map/all_gather | solution.py:39
  107.2 13.5 %gather_fusion.1 = bf16[2048,16]{1,0:T(8,128)(2,1)S(1)} fusion(bf16[65536,16]{1,0:T(8,128)(2,1)} %all-gather.6.cloned.1.call-done, s32[2048]{0:T(1024)S(1)} %broadcast_clamp_fusion), kind=kCustom, calls=%fused_computation.1 | custom fusion | bytes 139264 | tf_op jit(solution)/shard_map/gather | solution.py:43
  120.8 0.3 broadcast_select_fusion
  121.1 0.2 copy.28
  121.3 0.1 copy_bitcast_fusion
  121.4 2.0 gather_fusion.2
  123.4 0.0 copy-start.3
  123.4 8.9 %fusion.1 = bf16[64,128,16]{1,2,0:T(8,128)(2,1)} fusion(bf16[64,8,128,128]{3,2,1,0:T(8,128)(2,1)} %bitcast.59, bf16[64,8,128,16]{2,3,1,0:T(8,128)(2,1)S(1)} %bitcast.58, f32[64,128]{1,0:T(8,128)S(1)} %bitcast_reduce_fusion), kind=kOutput, calls=%fused_computation.10 | convolution fusion | flops 268697600 | bytes 19169280 | tf_op jit(solution)/shard_map/tkab,tkbf->taf/dot_general | solution.py:52
  132.3 0.0 all-to-all-done
  132.3 15.7 %all-to-all-start.1 = ((bf16[64,128,16]{1,2,0:T(8,128)(2,1)}), bf16[64,128,16]{1,2,0:T(8,128)(2,1)S(1)}, u32[]{:S(2)}, u32[]{:S(2)}) async-start(bf16[64,128,16]{1,2,0:T(8,128)(2,1)} %fusion.1), calls=%async_computation.1 | async-start | bytes 524288 | tf_op jit(solution)/shard_map/all_to_all | solution.py:60
  148.0 0.2 all-reduce.3.cloned.1.call-start
  148.2 102.0 %all-gather.4.cloned.1.call-done = bf16[1024,512]{1,0:T(8,128)(2,1)} async-done(((bf16[16,512]{1,0:T(8,128)(2,1)}), bf16[1024,512]{1,0:T(8,128)(2,1)}) %all-gather.4.cloned.1.call-update) | async-done | bytes 1048592 | tf_op jit(solution)/shard_map/all_gather | solution.py:64
  250.2 1.5 fusion.8
  251.8 137.4 %all-gather.8.cloned.1.call-done = bf16[1024,512]{1,0:T(8,128)(2,1)} async-done(((bf16[16,512]{1,0:T(8,128)(2,1)}), bf16[1024,512]{1,0:T(8,128)(2,1)}) %all-gather.8.cloned.1.call-update) | async-done | bytes 1048592 | tf_op jit(solution)/shard_map/all_gather | solution.py:68
  389.2 0.0 all-to-all-done.1
  389.2 2.3 fusion.7
  391.5 1.0 stack.2
  392.5 365.5 %all_to_all.40 = bf16[64,128,512]{2,1,0:T(8,128)(2,1)S(1)} all-to-all(bf16[64,128,512]{2,1,0:T(8,128)(2,1)S(1)} %stack.2), channel_id=1, replica_groups=mesh['feat'=64,'dom'=8] {'feat'}, dimensions={0} | all-to-all | bytes 16777216 | tf_op jit(solution)/shard_map/all_to_all | solution.py:12
  757.9 1.8 convolution_bitcast_fusion.1
  759.8 2.8 convolution_bitcast_fusion.2
  762.5 0.0 all-reduce.3.cloned.1.call-update
  762.5 71.3 %all-reduce.3.cloned.1.call-done = (f32[16,512]{1,0:T(8,128)}, f32[16,512]{1,0:T(8,128)}) async-done(((f32[16,512]{1,0:T(8,128)}, f32[16,512]{1,0:T(8,128)}), (f32[16,512]{1,0:T(8,128)}, f32[16,512]{1,0:T(8,128)})) %all-reduce.3.cloned.1.call-update) | async-done | bytes 65552 | tf_op jit(solution)/shard_map/psum | solution.py:80
  833.8 1.4 copy.39
  835.2 1.4 copy.40
  (13 shorter events, 0.1 us)
Async XLA Ops:
  7.2 24.8 %copy-start = (s32[8,8,256]{2,1,0:T(8,128)S(1)}, s32[8,8,256]{2,1,0:T(8,128)}, u32[]{:S(2)}) copy-start(s32[8,8,256]{2,1,0:T(8,128)} %param.13) | copy-start | bytes 196612
  7.2 30.2 %copy-start.1 = (bf16[64,128,128]{2,1,0:T(8,128)(2,1)S(1)}, bf16[64,128,128]{2,1,0:T(8,128)(2,1)}, u32[]{:S(2)}) copy-start(bf16[64,128,128]{2,1,0:T(8,128)(2,1)} %param.17) | copy-start | bytes 6291460
  7.2 100.0 %all-gather.6.cloned.1.call-start = ((), (), s32[]{:S(2)}) async-start(), calls=%async_computation.4 | async-start | bytes 18874368 | tf_op jit(solution)/shard_map/all_gather | solution.py:39
  10.0 240.2 %all-gather.4.cloned.1.call-start = ((), (), s32[]{:S(2)}) async-start(), calls=%async_computation.3 | async-start | bytes 1064960 | tf_op jit(solution)/shard_map/all_gather | solution.py:64
  12.5 119.8 %all-to-all-start = ((bf16[64,128,16]{1,2,0:T(8,128)(2,1)}), bf16[64,128,16]{1,2,0:T(8,128)(2,1)S(1)}, u32[]{:S(2)}, u32[]{:S(2)}) async-start(bf16[64,128,16]{1,2,0:T(8,128)(2,1)} %copy_bitcast_fusion.1), calls=%async_computation | async-start | bytes 524288 | tf_op jit(solution)/shard_map/all_to_all | solution.py:59
  31.1 358.0 %all-gather.8.cloned.1.call-start = ((), (), s32[]{:S(2)}) async-start(), calls=%async_computation.5 | async-start | bytes 1064960 | tf_op jit(solution)/shard_map/all_gather | solution.py:68
  51.4 69.9 %copy-start.2 = (bf16[8192,16]{0,1:T(8,128)(2,1)S(1)}, bf16[8192,16]{0,1:T(8,128)(2,1)}, u32[]{:S(2)}) copy-start(bf16[8192,16]{0,1:T(8,128)(2,1)} %param.9) | copy-start | bytes 786436
  123.4 265.8 %copy-start.3 = (bf16[128,512]{1,0:T(8,128)(2,1)S(1)}, bf16[128,512]{1,0:T(8,128)(2,1)}, u32[]{:S(2)}) copy-start(bf16[128,512]{1,0:T(8,128)(2,1)} %param.12) | copy-start | bytes 393220
  132.3 256.9 %all-to-all-start.1 = ((bf16[64,128,16]{1,2,0:T(8,128)(2,1)}), bf16[64,128,16]{1,2,0:T(8,128)(2,1)S(1)}, u32[]{:S(2)}, u32[]{:S(2)}) async-start(bf16[64,128,16]{1,2,0:T(8,128)(2,1)} %fusion.1), calls=%async_computation.1 | async-start | bytes 524288 | tf_op jit(solution)/shard_map/all_to_all | solution.py:60
  148.0 685.8 %all-reduce.3.cloned.1.call-start = ((), (), s32[]{:S(2)}) async-start(), calls=%async_computation.6 | async-start | bytes 131072 | tf_op jit(solution)/shard_map/psum | solution.py:80
Sparse Core Ops, SparseCore 0:
  10.2 97.0 all-gather.5
  110.2 140.0 all-gather.3
  253.2 135.9 all-gather.7
  762.7 71.1 all-reduce.2
